TPU v7x, 32 devices: a whole 2x2x4 slice. The times are simulated.
32 devices in a mesh: section: 4 (over z), dp: 4 (over x, core), mp: 2 (over y).
Axes of the slice: x: 2, y: 2, z: 4, core: 2. Of those that a mesh axis runs over, the one named last changes fastest.
Arguments:
- hidden: bfloat16 [4, 16, 4, 4096], P('section', 'mp', 'dp'), may hold values from -2048 to 2048
- token_ids: int32 [16, 4], P('mp', 'dp'), may hold values from 0 to 8191
- seq_lengths: int32 [4], replicated, may hold values from 1 to 16, 21 in all
- head_slices: bfloat16 [4, 4096, 8192], P('section', None, ('dp', 'mp')), may hold values from -8 to 8
- value_head: bfloat16 [4, 4096], P('section'), may hold values from -0.09375 to 0.09375
Outputs:
- scores: float32 [4, 16, 4], P('section', 'mp', 'dp')
- advantages: float32 [16, 4], P('mp', 'dp')
- trunk_grad: bfloat16 [4, 16, 4, 4096], P('section', 'mp', 'dp')
Inputs may be any that keep to these rules, and one draw needn't show every extreme that they name: Sequence j is live at positions 0 to seq_lengths[j] - 1; the lengths sum to 21 and one of them is 16.
All inputs are finite; a program needn't handle non-finite values.
Results may differ from a plain program's by a relative error of at most 0.0047.
Values may be sent and summed in bfloat16 or wider, within the bound.
A program may use at most 64 MiB of HBM per device.

v0:
```python
import math

import jax
import jax.numpy as jnp
from jax import lax
from jax.sharding import PartitionSpec as P

gae_decay = 0.95
reward_gain = 0.5
drift_gain = 0.1
penalty_gain = 0.2
loss_scale = 16.0


def from_root(value, axis, source):
    kept = jnp.where(lax.axis_index(axis) == source, value, 0).astype(value.dtype)
    return lax.psum(kept, axis)


def joined(x, axis, combine):
    everything = jax.tree.map(lambda part: lax.all_gather(part, axis), x)
    first = jax.tree.map(lambda part: part[0], everything)

    def turn(k, so_far):
        return combine(so_far, jax.tree.map(lambda part: part[k], everything))

    return lax.fori_loop(1, lax.axis_size(axis), turn, first)


def block_logits(gathered, head_part):
    return jnp.dot(gathered, head_part, preferred_element_type=jnp.float32)


def merge_parts(earlier_part, later_part):
    maximum = jnp.maximum(earlier_part[0], later_part[0])
    exp_total = earlier_part[1] * jnp.exp(earlier_part[0] - maximum) + later_part[1] * jnp.exp(
        later_part[0] - maximum
    )
    return (maximum, exp_total, earlier_part[2] + later_part[2])


def local(hidden, token_ids, seq_lengths, head_slices, value_head):
    sections = lax.axis_size("section")
    per_device = hidden.shape[1]
    model_width = hidden.shape[3]
    vocab_part = head_slices.shape[2]
    seq_count = seq_lengths.shape[0]
    length = per_device * lax.axis_size("mp")
    head_part = head_slices[0]
    critic_head = value_head[0]
    own_block = from_root(hidden, "section", 0)
    gathered, row_ids = (
        lax.all_gather(own_block[0, :, 0, :], ("dp", "mp"), axis=0, tiled=True),
        lax.all_gather(token_ids[:, 0], ("dp", "mp"), axis=0, tiled=True),
    )
    row_total = gathered.shape[0]
    row_iota = lax.broadcasted_iota(jnp.int32, (row_total,), 0)
    seq_of = row_iota // length
    pos_of = row_iota % length
    seq_table = lax.broadcasted_iota(jnp.int32, (row_total, seq_count), 1)
    length_of = jnp.sum(jnp.where(seq_of[:, None] == seq_table, seq_lengths[None, :], 0), axis=1)
    live_bool = pos_of < length_of
    live_mask = live_bool.astype(jnp.float32)
    logits = block_logits(gathered, head_part)
    own_index = lax.axis_index("dp") * lax.axis_size("mp") + lax.axis_index("mp")
    vocab_start = own_index * vocab_part
    column = lax.broadcasted_iota(jnp.int32, logits.shape, 1) + vocab_start
    maximum = jnp.max(logits, axis=1)
    exp_total = jnp.sum(jnp.exp(logits - maximum[:, None]), axis=1)
    picked = jnp.sum(jnp.where(column == row_ids[:, None], logits, jnp.float32(0.0)), axis=1)
    values = jnp.dot(gathered, critic_head, preferred_element_type=jnp.float32)
    maximum, exp_total, picked = joined((maximum, exp_total, picked), ("dp", "mp"), merge_parts)
    normal = maximum + jnp.log(exp_total)
    scored = jnp.where(live_bool, picked - normal, jnp.float32(0.0))
    own_start = own_index * per_device
    scores_out = lax.dynamic_slice_in_dim(scored, own_start, per_device, 0).reshape(
        1, per_device, 1
    )
    joined_scores, joined_values = (
        lax.all_gather(scored[None, :], "section", axis=0, tiled=True),
        lax.all_gather(values[None, :], "section", axis=0, tiled=True),
    )
    behaviour = joined_scores[0]
    implicit = joined_scores[1]
    anchor = joined_scores[2]
    current = joined_scores[3]
    reward = (reward_gain * (implicit - anchor) - drift_gain * (behaviour - anchor)).reshape(
        seq_count, length
    )
    critic_grid = joined_values[1].reshape(seq_count, length)
    live_grid = live_mask.reshape(seq_count, length)
    next_values = jnp.concatenate(
        [critic_grid[:, 1:], jnp.zeros((seq_count, 1), jnp.float32)], axis=1
    )
    next_mask = jnp.concatenate([live_grid[:, 1:], jnp.zeros((seq_count, 1), jnp.float32)], axis=1)
    td_error = live_grid * (reward + next_mask * next_values - critic_grid)
    later_pos = lax.broadcasted_iota(jnp.int32, (length, length), 0)
    earlier = lax.broadcasted_iota(jnp.int32, (length, length), 1)
    weights_t = jnp.where(
        later_pos >= earlier,
        jnp.exp((later_pos - earlier).astype(jnp.float32) * math.log(gae_decay)),
        jnp.float32(0.0),
    )
    advantage = jnp.dot(td_error, weights_t, precision=lax.Precision.HIGHEST).reshape(row_total)
    advantage_out = lax.dynamic_slice_in_dim(advantage, own_start, per_device, 0).reshape(
        per_device, 1
    )
    prob_ratio = jnp.exp(current - behaviour)
    token_grad = (
        -(loss_scale / seq_count)
        * live_mask
        * (prob_ratio * advantage - penalty_gain * (prob_ratio - 1.0))
    )
    soft_probs = jnp.exp(logits - normal[:, None])
    target_hit = (column == row_ids[:, None]).astype(jnp.float32)
    slope = (token_grad[:, None] * (target_hit - soft_probs)).astype(jnp.bfloat16)
    grad_rows = lax.psum_scatter(
        lax.dot_general(
            slope, head_part, (((1,), (1,)), ((), ())), preferred_element_type=jnp.float32
        ),
        ("dp", "mp"),
        scatter_dimension=0,
        tiled=True,
    )
    learner = (lax.axis_index("section") == sections - 1).astype(jnp.float32)
    trunk_out = (grad_rows * learner).astype(jnp.bfloat16).reshape(1, per_device, 1, model_width)
    return (scores_out, advantage_out, trunk_out)


def solution(mesh):
    return jax.shard_map(
        local,
        mesh=mesh,
        in_specs=(
            P("section", "mp", "dp", None),
            P("mp", "dp"),
            P(),
            P("section", None, ("dp", "mp")),
            P("section", None),
        ),
        out_specs=(P("section", "mp", "dp"), P("mp", "dp"), P("section", "mp", "dp", None)),
        check_vma=False,
    )
```

profile of v0, /device:TPU:0, one launch (start us, length us, event | category | flops | bytes accessed | tf_op | source)
XLA Modules:
  0.0 146.0 jit_solution(6107833239940460607)
XLA Ops:
  7.2 0.0 copy-start
  7.2 0.0 all-reduce.12.cloned.1.call-start
  7.2 1.5 %select_bitcast_fusion = bf16[8,4096]{1,0:T(8,128)(2,1)} fusion(bf16[1,8,1,4096]{3,1,2,0:T(8,128)(2,1)} %param.7, pred[]{:T(512)S(6)} %eq.30), kind=kLoop, calls=%fused_computation.28 | loop fusion | flops 32768 | bytes 131073 | tf_op jit(solution)/shard_map/squeeze | solution.py:53
  8.7 0.0 all-reduce.12.cloned.1.call-update
  8.7 0.0 reduce-scatter.2.cloned.1.call-start
  8.8 1.2 dynamic-slice.4
  10.1 1.2 dynamic-slice
  13.2 0.8 bitcast_dynamic-update-slice_fusion
  14.0 8.8 %all-reduce.4 = s32[64]{0:T(128)S(1)} all-reduce(s32[64]{0:T(128)S(1)} %bitcast_dynamic-update-slice_fusion), channel_id=4, replica_groups=mesh['section'=4,'dp'=4,'mp'=2] {'dp','mp'}, use_global_device_ids=true, to_apply=%add.4 | all-reduce | flops 64 | bytes 512
  22.8 0.7 select_reduce_fusion
  23.5 0.1 reduce_sum.32
  23.6 0.1 slice.37
  23.7 24.2 %all-reduce.12.cloned.1.call-done = bf16[8,4096]{1,0:T(8,128)(2,1)} async-done(((bf16[8,4096]{1,0:T(8,128)(2,1)}), bf16[8,4096]{1,0:T(8,128)(2,1)}) %all-reduce.12.cloned.1.call-update) | async-done | bytes 65552 | tf_op jit(solution)/shard_map/psum | solution.py:17
  47.9 16.6 %all_gather.30 = bf16[64,4096]{1,0:T(8,128)(2,1)S(1)} all-gather(bf16[8,4096]{1,0:T(8,128)(2,1)} %all-reduce.12.cloned.1.call-done), channel_id=1, replica_groups=mesh['section'=4,'dp'=4,'mp'=2] {'dp','mp'}, dimensions={0}, use_global_device_ids=true | all-gather | bytes 589824 | tf_op jit(solution)/shard_map/all_gather | solution.py:53
  64.5 5.1 %fusion.45 = (f32[64]{0:T(128)S(1)}, f32[64,1024]{1,0:T(8,128)S(1)}) fusion(bf16[64,4096]{1,0:T(8,128)(2,1)S(1)} %all_gather.30, bf16[1,4096,1024]{2,1,0:T(8,128)(2,1)} %param.10), kind=kOutput, calls=%fused_computation.72 | convolution fusion | flops 536936384 | bytes 9175296 | tf_op jit(solution)/shard_map/dot_general | solution.py:31
  69.5 0.2 dynamic-update-slice
  69.8 0.2 fusion.11
  70.0 0.2 dynamic-update-slice.3
  70.3 0.2 dynamic-update-slice.1
  70.5 14.3 %all-reduce.8 = (f32[512]{0:T(512)S(1)}, f32[512]{0:T(512)S(1)}, f32[512]{0:T(512)S(1)}) all-reduce(f32[512]{0:T(512)S(1)} %dynamic-update-slice, f32[512]{0:T(512)S(1)} %dynamic-update-slice.1, f32[512]{0:T(512)S(1)} %dynamic-update-slice.3), channel_id=2, replica_groups=mesh['section'=4,'dp'=4,'mp'=2] {'dp','mp'}, use_global_device_ids=true, to_apply=%add.2 | all-reduce | flops 1536 | bytes 12288
  84.7 0.1 reshape.90
  84.8 0.1 reshape.88
  84.9 0.1 reshape.87
  85.0 0.0 copy-done
  85.0 0.2 convolution_bitcast_fusion
  85.2 0.3 while.19
  85.5 0.2 dynamic-update-slice.5
  85.8 0.1 fusion.44
  85.9 10.4 %all-reduce.9 = (f32[256]{0:T(256)S(1)}, f32[256]{0:T(256)S(1)}) all-reduce(f32[256]{0:T(256)S(1)} %dynamic-update-slice.5, f32[256]{0:T(256)S(1)} %get-tuple-element.207), channel_id=7, replica_groups=mesh['section'=4,'dp'=4,'mp'=2] {'section'}, use_global_device_ids=true, to_apply=%add.7 | all-reduce | flops 512 | bytes 4096
  96.3 0.1 slice.47
  96.4 0.1 multiply_subtract_fusion
  96.5 0.1 reshape_squeeze.3
  96.5 0.1 sub.97
  96.6 0.1 slice.39
  96.7 0.1 fusion.26
  96.8 0.1 reshape.84
  96.9 0.1 subtract_multiply_fusion
  97.0 7.1 %fusion.7 = f32[64,4096]{1,0:T(8,128)} fusion(bf16[1,4096,1024]{2,1,0:T(8,128)(2,1)} %param.10, f32[64,1024]{1,0:T(8,128)S(1)} %get-tuple-element.212, f32[64]{0:T(128)S(1)} %get-tuple-element.209, f32[64]{0:T(128)S(1)} %subtract_multiply_fusion, s32[1024]{0:T(1024)S(1)} %iota_add_fusion, s32[64]{0:T(128)S(1)} %all-reduce.4), kind=kOutput, calls=%fused_computation.10 | convolution fusion | flops 537264128 | bytes 9704192 | tf_op jit(solution)/shard_map/dot_general | solution.py:118
  104.1 0.0 reduce-scatter.2.cloned.1.call-update
  104.1 0.6 dynamic-slice_bitcast_fusion
  104.7 0.6 dynamic-slice_bitcast_fusion.1
  105.3 32.4 %reduce-scatter.2.cloned.1.call-done = f32[8,4096]{1,0:T(8,128)} async-done(((f32[64,4096]{1,0:T(8,128)}), f32[8,4096]{1,0:T(8,128)}) %reduce-scatter.2.cloned.1.call-update) | async-done | bytes 131088 | tf_op jit(solution)/shard_map/reduce_scatter | solution.py:117
  137.7 1.5 %fusion.20 = bf16[1,8,1,4096]{3,1,2,0:T(8,128)(2,1)} fusion(f32[8,4096]{1,0:T(8,128)} %reduce-scatter.2.cloned.1.call-done, f32[]{:T(128)S(6)} %convert_element_type.22), kind=kLoop, calls=%fused_computation.27 | loop fusion | flops 65536 | bytes 196612 | tf_op jit(solution)/shard_map/reshape | solution.py:126
  (19 shorter events, 0.2 us)
Async XLA Ops:
  7.2 77.8 %copy-start = (bf16[1,4096]{1,0:T(2,128)(2,1)S(1)}, bf16[1,4096]{1,0:T(2,128)(2,1)}, u32[]{:S(2)}) copy-start(bf16[1,4096]{1,0:T(2,128)(2,1)} %param.11) | copy-start | bytes 24580
  7.2 40.7 %all-reduce.12.cloned.1.call-start = ((), (), s32[]{:S(2)}) async-start(), calls=%async_computation.1 | async-start | bytes 131072 | tf_op jit(solution)/shard_map/psum | solution.py:17
  8.7 128.9 %reduce-scatter.2.cloned.1.call-start = ((), (), s32[]{:S(2)}) async-start(), calls=%async_computation.2 | async-start | bytes 1179648 | tf_op jit(solution)/shard_map/reduce_scatter | solution.py:117
Sparse Core Ops, SparseCore 0:
  10.9 37.0 all-reduce.11
  104.2 33.4 reduce-scatter.1
where the time goes:
time: 146 us
  waiting for transfers between devices  56.6 us (39%)
  blocking collectives  50.1 us (34%)
  between operations  16 us (11%)
  matrix products  12.5 us (9%)
  local copies, waits for them, and re-layouts  6.16 us (4%)
  other arithmetic  4.46 us (3%)
    unnamed x3, blocking collectives  33.5 us
    reduce_scatter x1, waiting for transfers between devices, local(): lax.psum_scatter(lax.dot_general(slope, head_part, (((1,), (1,)), ((), ()...  32.4 us
    psum x1, waiting for transfers between devices, from_root(): return lax.psum(kept, axis)  24.2 us
    all_gather x1, blocking collectives, local(): lax.all_gather(own_block[0, :, 0, :], ('dp', 'mp'), axis=0, tiled=True)  16.6 us
    dot_general x1, matrix products, local(): lax.dot_general(slope, head_part, (((1,), (1,)), ((), ())), preferred_ele...  7.06 us
    dot_general x1, matrix products, block_logits(): return jnp.dot(gathered, head_part, preferred_element_type=jnp.float32)  5.06 us
    unnamed x14, local copies, waits for them, and re-layouts  4.19 us
  transfers between devices with their start and end apart: 2, of which 2 were waited for; matrix products, arithmetic and copies ran while one was open for 4% of the time, Pallas kernels for 0%

commit v1 on v0

v1 whole, which is shorter than its diff:
```python
import functools
import math

import jax
import jax.numpy as jnp
from jax import lax
from jax.experimental import pallas as pl
from jax.experimental.pallas import tpu as pltpu
from jax.sharding import PartitionSpec as P

gae_decay = 0.95
reward_gain = 0.5
drift_gain = 0.1
penalty_gain = 0.2
loss_scale = 16.0

MESH = pl.DeviceIdType.MESH
f32 = jnp.float32
bf16 = jnp.bfloat16


def each(count, fn):
    if count <= 9:
        for o in range(1, count):
            fn(o)
    else:
        lax.fori_loop(1, count, lambda o, carry: (fn(o), carry)[1], 0)


def kernel(
    cfg,
    hid_ref,
    tok_ref,
    len_ref,
    head_ref,
    vh_ref,
    score_out,
    adv_out,
    trunk_out,
    head_v,
    buf,
    tokbuf,
    statbuf,
    zbuf,
    ab,
    pf,
    s1,
    r1,
    s2,
    r2,
    hid_sem,
    head_sem,
    zrow_s,
    zrow_r,
    row_s,
    row_r,
    tok_s,
    tok_r,
    stat_s,
    stat_r,
    zs_s,
    zs_r,
    r1_s,
    r1_r,
    r2_s,
    r2_r,
):
    S, DP, MP, per, D, V, SEQ, C, C2, TILE = cfg
    PL = DP * MP
    G = PL // 2
    R = PL * per
    Rp = statbuf.shape[2]
    LEN = per * MP
    Kc = D // C
    Dc = D // C2
    sec = lax.axis_index("section")
    dp = lax.axis_index("dp")
    mp = lax.axis_index("mp")
    core = lax.rem(dp, 2)
    q = dp * MP + mp
    g = (dp // 2) * MP + mp
    partner = {"dp": dp + 1 - 2 * core, "mp": mp}
    partner_q = (dp + 1 - 2 * core) * MP + mp

    def plane_dev(o):
        i = lax.rem(q + o, PL)
        return {"dp": i // MP, "mp": lax.rem(i, MP)}, i

    def chip_dev(o, which):
        i = lax.rem(g + o, G)
        d = (i // MP) * 2 + which
        m = lax.rem(i, MP)
        return {"dp": d, "mp": m}, d * MP + m, i

    def sec_dev(o):
        i = lax.rem(sec + o, S)
        return {"section": i}, i

    def rc(src, dst, ss, rs, dev):
        return pltpu.make_async_remote_copy(
            src_ref=src, dst_ref=dst, send_sem=ss, recv_sem=rs, device_id=dev, device_id_type=MESH
        )

    def head_copy(c):
        cut = pl.ds(c * Kc, Kc)
        return pltpu.make_async_copy(head_ref.at[0, cut, :], head_v.at[cut, :], head_sem.at[c])

    hid_copy = pltpu.make_async_copy(hid_ref, buf.at[q], hid_sem)

    @pl.when(sec == 0)
    def _():
        hid_copy.start()

    for c in range(C):
        head_copy(c).start()

    tokbuf[q] = jnp.broadcast_to(tok_ref[...], (per, 128))

    barrier = pltpu.get_barrier_semaphore()

    def greet_plane(o):
        pl.semaphore_signal(barrier, inc=1, device_id=plane_dev(o)[0], device_id_type=MESH)

    def greet_section(o):
        pl.semaphore_signal(barrier, inc=1, device_id=sec_dev(o)[0], device_id_type=MESH)

    each(S, greet_section)
    each(PL, greet_plane)
    pl.semaphore_wait(barrier, PL - 1 + S - 1)

    def piece(slot, c):
        return buf.at[slot, :, pl.ds(c * Kc, Kc)]

    def z_copy(c, s):
        return rc(piece(q, c), piece(q, c), zrow_s.at[c, s], zrow_r.at[c], {"section": s})

    def own_to_partner(c):
        return rc(piece(q, c), piece(q, c), row_s.at[c, 0], row_r.at[c, q], partner)

    def own_to_chip(c, o):
        return rc(piece(q, c), piece(q, c), row_s.at[c, o], row_r.at[c, q], chip_dev(o, core)[0])

    def forward(c, o):
        i = chip_dev(o, core)[1]
        return rc(piece(i, c), piece(i, c), row_s.at[c, G - 1 + o], row_r.at[c, i], partner)

    def arrived(c, i):
        rc(piece(i, c), piece(i, c), row_s.at[c, 0], row_r.at[c, i], partner).wait_recv()

    def tok_copy(o):
        return rc(tokbuf.at[q], tokbuf.at[q], tok_s.at[o], tok_r.at[q], plane_dev(o)[0])

    def spread(c):
        @pl.when(sec == 0)
        def _():
            for s in range(S - 1, 0, -1):
                z_copy(c, s).start()

        @pl.when(sec != 0)
        def _():
            z_copy(c, 0).wait_recv()

        each(G, lambda o: own_to_chip(c, o).start())
        own_to_partner(c).start()

    def relay(c):
        def one(o):
            arrived(c, chip_dev(o, core)[1])
            forward(c, o).start()

        each(G, one)

    def settle(c):
        arrived(c, partner_q)
        each(G, lambda o: arrived(c, chip_dev(o, 1 - core)[1]))

    @pl.when(sec == 0)
    def _():
        hid_copy.wait()

    logits = jnp.zeros((R, V), f32)
    values = jnp.zeros((R, 1), f32)
    for step in range(C + 2):
        if step < C:
            spread(step)
        if step == 0:
            each(PL, lambda o: tok_copy(o).start())
        if 0 <= step - 1 < C:
            relay(step - 1)
        c = step - 2
        if c >= 0:
            settle(c)
            head_copy(c).wait()
            x = buf[:, :, c * Kc : (c + 1) * Kc].astype(f32).reshape(R, Kc)
            logits = logits + jnp.dot(
                x.astype(bf16), head_v[c * Kc : (c + 1) * Kc, :], preferred_element_type=f32
            )
            values = values + jnp.sum(
                x * vh_ref[:, c * Kc : (c + 1) * Kc].astype(f32), axis=1, keepdims=True
            )

    def tok_arrived(o):
        i = plane_dev(o)[1]
        rc(tokbuf.at[i], tokbuf.at[i], tok_s.at[o], tok_r.at[i], plane_dev(o)[0]).wait_recv()

    each(PL, tok_arrived)

    ids = tokbuf[...].reshape(R, 128)[:, :1] - q * V
    hit = lax.broadcasted_iota(jnp.int32, (R, V), 1) == ids
    m_col = jnp.max(logits, axis=1, keepdims=True)
    e = jnp.exp(logits - m_col)
    l_col = jnp.sum(e, axis=1, keepdims=True)
    p_col = jnp.sum(jnp.where(hit, logits, 0.0), axis=1, keepdims=True)
    eye = lax.broadcasted_iota(jnp.int32, (R, Rp), 0) == lax.broadcasted_iota(
        jnp.int32, (R, Rp), 1
    )

    def to_lanes(col):
        return jnp.sum(jnp.where(eye, col, 0.0), axis=0, keepdims=True)

    def to_column(row):
        return jnp.sum(jnp.where(eye, row, 0.0), axis=1, keepdims=True)

    sub = lax.broadcasted_iota(jnp.int32, (8, Rp), 0)
    m_lane = to_lanes(m_col)
    statbuf[q] = jnp.where(
        sub == 0, m_lane, jnp.where(sub == 1, to_lanes(l_col), to_lanes(p_col))
    )

    def stat_copy(o):
        return rc(statbuf.at[q], statbuf.at[q], stat_s.at[o], stat_r.at[q], plane_dev(o)[0])

    each(PL, lambda o: stat_copy(o).start())

    @pl.when(sec == S - 1)
    def _():
        both = jnp.concatenate(
            [jnp.where(hit, 0.0, e).astype(bf16), hit.astype(f32).astype(bf16)], axis=0
        )

        def tile(t, carry):
            cut = pl.ds(pl.multiple_of(t * TILE, TILE), TILE)
            ab[:, cut] = lax.dot_general(
                both, head_v[cut, :], (((1,), (1,)), ((), ())), preferred_element_type=f32
            )
            return carry

        lax.fori_loop(0, D // TILE, tile, 0)

    def stat_arrived(o):
        dev, i = plane_dev(o)
        rc(statbuf.at[i], statbuf.at[i], stat_s.at[o], stat_r.at[i], dev).wait_recv()

    each(PL, stat_arrived)
    st = statbuf[...]
    m_all = st[:, 0:1, :]
    m_top = jnp.max(m_all, axis=0)
    l_top = jnp.sum(st[:, 1:2, :] * jnp.exp(m_all - m_top[None]), axis=0)
    picked = jnp.sum(st[:, 2:3, :], axis=0)
    log_norm = m_top + jnp.log(l_top)
    raw = picked - log_norm

    lane = lax.broadcasted_iota(jnp.int32, (1, Rp), 1)
    seq_of = lane // LEN
    length_of = jnp.zeros((1, Rp), jnp.int32)
    for j in range(SEQ):
        length_of = length_of + jnp.where(seq_of == j, len_ref[j], 0)
    live = (lane - seq_of * LEN) < length_of
    scored = jnp.where(live, raw, 0.0)
    zbuf[sec] = jnp.where(sub == 0, scored, to_lanes(values))

    def zs_copy(o):
        return rc(zbuf.at[sec], zbuf.at[sec], zs_s.at[o], zs_r.at[sec], sec_dev(o)[0])

    each(S, lambda o: zs_copy(o).start())

    def s2_copy(c, o):
        dev, _, i = chip_dev(o, core)
        return rc(s2.at[c, i], r2.at[c, g], r2_s.at[c, o], r2_r.at[c, g], dev)

    @pl.when(sec == S - 1)
    def _():
        s_col = to_column(jnp.exp(m_lane - log_norm))
        t_col = to_column(1.0 - jnp.exp(raw))
        for c in range(C2):
            cut = slice(c * Dc, (c + 1) * Dc)
            pf[c] = (t_col * ab[R:, cut] - s_col * ab[:R, cut]).reshape(
                DP // 2, 2, MP, per, Dc
            )
            for i in range(DP // 2):
                s1[c, i * MP : (i + 1) * MP] = pf[c, i, 1 - core].astype(bf16)
            rc(s1.at[c], r1.at[c], r1_s.at[c], r1_r.at[c], partner).start()
        for c in range(C2):
            rc(s1.at[c], r1.at[c], r1_s.at[c], r1_r.at[c], partner).wait_recv()
            for i in range(DP // 2):
                s2[c, i * MP : (i + 1) * MP] = (
                    pf[c, i, core] + r1[c, i * MP : (i + 1) * MP].astype(f32)
                ).astype(bf16)
            each(G, lambda o: s2_copy(c, o).start())

    def zs_arrived(o):
        dev, i = sec_dev(o)
        rc(zbuf.at[i], zbuf.at[i], zs_s.at[o], zs_r.at[i], dev).wait_recv()

    each(S, zs_arrived)
    behaviour = zbuf[0][0:1]
    implicit = zbuf[1][0:1]
    anchor = zbuf[2][0:1]
    current = zbuf[S - 1][0:1]
    critic = jnp.where(live, zbuf[1][1:2], 0.0)
    reward = reward_gain * (implicit - anchor) - drift_gain * (behaviour - anchor)
    base = jnp.where(live, reward - critic, 0.0)
    later = lax.broadcasted_iota(jnp.int32, (Rp, Rp), 0)
    earlier = lax.broadcasted_iota(jnp.int32, (Rp, Rp), 1)
    gap = later - earlier
    same = (later // LEN) == (earlier // LEN)
    decay = math.log(gae_decay)
    weights = jnp.where(same & (gap >= 0), jnp.exp(gap.astype(f32) * decay), 0.0)
    shifted = jnp.where(same & (gap >= 1), jnp.exp((gap - 1).astype(f32) * decay), 0.0)
    advantage = (
        jnp.dot(
            jnp.broadcast_to(base, (8, Rp)),
            weights,
            precision=lax.Precision.HIGHEST,
            preferred_element_type=f32,
        )
        + jnp.dot(
            jnp.broadcast_to(critic, (8, Rp)),
            shifted,
            precision=lax.Precision.HIGHEST,
            preferred_element_type=f32,
        )
    )[0:1]
    prob_ratio = jnp.exp(current - behaviour)
    coeff = jnp.where(
        live,
        -(loss_scale / SEQ) * (prob_ratio * advantage - penalty_gain * (prob_ratio - 1.0)),
        0.0,
    )
    own = lax.broadcasted_iota(jnp.int32, (per, Rp), 1) == (
        lax.broadcasted_iota(jnp.int32, (per, Rp), 0) + q * per
    )

    def own_column(row):
        return jnp.sum(jnp.where(own, row, 0.0), axis=1, keepdims=True)

    score_out[0] = own_column(scored)
    adv_out[...] = own_column(advantage)

    @pl.when(sec != S - 1)
    def _():
        trunk_out[...] = jnp.zeros_like(trunk_out)

    @pl.when(sec == S - 1)
    def _():
        factor = own_column(coeff)
        for c in range(C2):

            def r2_arrived(o):
                dev, _, i = chip_dev(o, core)
                rc(s2.at[c, i], r2.at[c, i], r2_s.at[c, o], r2_r.at[c, i], dev).wait_recv()

            each(G, r2_arrived)
            total = pf[c, dp // 2, core, mp] + r1[c, g].astype(f32)
            if G <= 9:
                for o in range(1, G):
                    total = total + r2[c, chip_dev(o, core)[2]].astype(f32)
            else:
                total = lax.fori_loop(
                    1, G, lambda o, t: t + r2[c, chip_dev(o, core)[2]].astype(f32), total
                )
            trunk_out[:, c * Dc : (c + 1) * Dc] = (total * factor).astype(bf16)
        for c in range(C2):
            rc(s1.at[c], r1.at[c], r1_s.at[c], r1_r.at[c], partner).wait_send()
            each(G, lambda o: s2_copy(c, o).wait_send())

    for c in range(C):

        @pl.when(sec == 0)
        def _():
            for s in range(1, S):
                z_copy(c, s).wait_send()

        own_to_partner(c).wait_send()
        each(G, lambda o: own_to_chip(c, o).wait_send())
        each(G, lambda o: forward(c, o).wait_send())
    each(PL, lambda o: tok_copy(o).wait_send())
    each(PL, lambda o: stat_copy(o).wait_send())
    each(S, lambda o: zs_copy(o).wait_send())


def local(hidden, token_ids, seq_lengths, head_slices, value_head):
    S = lax.axis_size("section")
    DP = lax.axis_size("dp")
    MP = lax.axis_size("mp")
    PL = DP * MP
    G = PL // 2
    per, D = hidden.shape[1], hidden.shape[3]
    V = head_slices.shape[2]
    SEQ = seq_lengths.shape[0]
    C, C2 = 4, 2
    TILE = min(512, D)
    R = PL * per
    Rp = -(-R // 128) * 128
    dma = pltpu.SemaphoreType.DMA
    vmem = pl.BlockSpec(memory_space=pltpu.VMEM)
    anym = pl.BlockSpec(memory_space=pl.ANY)
    scores, adv, trunk = pl.pallas_call(
        functools.partial(kernel, (S, DP, MP, per, D, V, SEQ, C, C2, TILE)),
        out_shape=(
            jax.ShapeDtypeStruct((1, per, 1), f32),
            jax.ShapeDtypeStruct((per, 1), f32),
            jax.ShapeDtypeStruct((per, D), bf16),
        ),
        in_specs=[anym, vmem, pl.BlockSpec(memory_space=pltpu.SMEM), anym, vmem],
        out_specs=(vmem, vmem, vmem),
        scratch_shapes=[
            pltpu.VMEM((D, V), bf16),
            pltpu.VMEM((PL, per, D), bf16),
            pltpu.VMEM((PL, per, 128), jnp.int32),
            pltpu.VMEM((PL, 8, Rp), f32),
            pltpu.VMEM((S, 8, Rp), f32),
            pltpu.VMEM((2 * R, D), f32),
            pltpu.VMEM((C2, DP // 2, 2, MP, per, D // C2), f32),
            pltpu.VMEM((C2, G, per, D // C2), bf16),
            pltpu.VMEM((C2, G, per, D // C2), bf16),
            pltpu.VMEM((C2, G, per, D // C2), bf16),
            pltpu.VMEM((C2, G, per, D // C2), bf16),
            dma(()),
            dma((C,)),
            dma((C, S)),
            dma((C,)),
            dma((C, 2 * G)),
            dma((C, PL)),
            dma((PL,)),
            dma((PL,)),
            dma((PL,)),
            dma((PL,)),
            dma((S,)),
            dma((S,)),
            dma((C2,)),
            dma((C2,)),
            dma((C2, G)),
            dma((C2, G)),
        ],
        compiler_params=pltpu.CompilerParams(
            collective_id=0, has_side_effects=True, vmem_limit_bytes=60 * 1024 * 1024
        ),
    )(hidden.reshape(per, D), token_ids, seq_lengths, head_slices, value_head)
    return scores, adv, trunk.reshape(1, per, 1, D)


def solution(mesh):
    return jax.shard_map(
        local,
        mesh=mesh,
        in_specs=(
            P("section", "mp", "dp", None),
            P("mp", "dp"),
            P(),
            P("section", None, ("dp", "mp")),
            P("section", None),
        ),
        out_specs=(P("section", "mp", "dp"), P("mp", "dp"), P("section", "mp", "dp", None)),
        check_vma=False,
    )
```

time: 146 us -> 35.2 us (0.24)
  waiting for transfers between devices: 56.6 us -> 0 us
  blocking collectives: 50.1 us -> 0 us
  Pallas kernels: 0 us -> 29 us
  between operations: 16 us -> 0.64 us
  matrix products: 12.5 us -> 0 us
  other arithmetic: 4.46 us -> 0 us
    unnamed x3 -> x0, blocking collectives: 33.5 us -> none
    reduce_scatter x1 -> x0, waiting for transfers between devices: 32.4 us -> none  [local(): lax.psum_scatter(lax.dot_general(slope, head_part, (((1,), (1,)), ((), ()...]
    pallas_call x0 -> x1, Pallas kernels: none -> 29 us  [local(): pl.pallas_call(functools.partial(kernel, (S, DP, MP, per, D, V, SEQ, C, C...]
    psum x1 -> x0, waiting for transfers between devices: 24.2 us -> none  [from_root(): return lax.psum(kept, axis)]
    all_gather x1 -> x0, blocking collectives: 16.6 us -> none  [local(): lax.all_gather(own_block[0, :, 0, :], ('dp', 'mp'), axis=0, tiled=True)]
    dot_general x4 -> x0, matrix products: 12.5 us -> none  [the longest x1 7.06 us: local(): lax.dot_general(slope, head_part, (((1,), (1,)), ((), ())), preferred_ele...]
    reshape x1 -> x0, other arithmetic: 1.54 us -> none  [local(): (grad_rows * learner).astype(jnp.bfloat16)]
    squeeze x1 -> x0, other arithmetic: 1.48 us -> none  [local(): own_block[0, :, 0, :]]
  transfers between devices with their start and end apart: 2 -> 0, of which waited for: 2 -> 0; matrix products, arithmetic and copies ran while one was open for 4% -> 0% of each run, Pallas kernels for 0% -> 0%
where the time goes in v1:
time: 35.2 us; the launch traced here: 34.9 us
  Pallas kernels  29 us (82%)
  local copies, waits for them, and re-layouts  5.33 us (15%)
  between operations  0.64 us (2%)
    pallas_call x1, Pallas kernels, local(): pl.pallas_call(functools.partial(kernel, (S, DP, MP, per, D, V, SEQ, C, C...  29 us
    unnamed x4, local copies, waits for them, and re-layouts  5.33 us

profile of v1, /device:TPU:0, one launch (start us, length us, event | category | flops | bytes accessed | tf_op | source)
XLA Modules:
  0.0 34.9 jit_solution(7297014543351564235)
XLA Ops:
  0.6 1.3 %copy.8.tok_ref = s32[8,1]{1,0:T(8,128)} copy(s32[8,1]{0,1:T(1,128)} %param.6) | data formatting | bytes 64 | tf_op args[1]
  2.0 29.0 %shard_map.76 = (f32[1,8,1]{2,1,0:T(8,128)}, f32[8,1]{1,0:T(8,128)}, bf16[8,4096]{1,0:T(8,128)(2,1)}) custom-call(bf16[8,4096]{1,0:T(8,128)(2,1)} %bitcast.2, s32[8,1]{1,0:T(8,128)} %copy.8.tok_ref, s32[4]{0:T(128)} %len_ref.1, bf16[1,4096,1024]{2,1,0:T(8,128)(2,1)} %head_ref.1, bf16[1,4096]{1,0:T(2,128)(2,1)} %vh_ref.1), custom_call_target="tpu_custom_call" | custom-call | tf_op jit(solution)/shard_map/pallas_call | solution.py:408
  30.9 1.3 %copy.9 = f32[1,8,1]{1,2,0:T(1,128)} copy(f32[1,8,1]{2,1,0:T(8,128)} %get-tuple-element.9) | data formatting | bytes 64
  32.2 1.3 %copy.10 = f32[8,1]{0,1:T(1,128)} copy(f32[8,1]{1,0:T(8,128)} %get-tuple-element.10) | data formatting | bytes 64
  33.4 1.5 %copy.12 = bf16[1,8,1,4096]{3,1,2,0:T(8,128)(2,1)} copy(bf16[1,8,1,4096]{3,1,2,0:T(8,128)(2,1)} %bitcast.3) | data formatting | bytes 131072

commit v2 on v1

--- a/solution.py
+++ b/solution.py
@@ -114,7 +114,11 @@
     for c in range(C):
         head_copy(c).start()
 
-    tokbuf[q] = jnp.broadcast_to(tok_ref[...], (per, 128))
+    corner = lax.broadcasted_iota(jnp.int32, (per, per), 0) == lax.broadcasted_iota(
+        jnp.int32, (per, per), 1
+    )
+    tok_col = jnp.sum(jnp.where(corner, tok_ref[...].astype(f32), 0.0), axis=1, keepdims=True)
+    tokbuf[q] = jnp.broadcast_to(tok_col.astype(jnp.int32), (per, 128))
 
     barrier = pltpu.get_barrier_semaphore()
 
@@ -344,8 +348,11 @@
     def own_column(row):
         return jnp.sum(jnp.where(own, row, 0.0), axis=1, keepdims=True)
 
-    score_out[0] = own_column(scored)
-    adv_out[...] = own_column(advantage)
+    def own_row(row):
+        return jnp.sum(jnp.where(corner, own_column(row), 0.0), axis=0, keepdims=True)
+
+    score_out[...] = own_row(scored)
+    adv_out[...] = own_row(advantage)
 
     @pl.when(sec != S - 1)
     def _():
@@ -398,7 +405,7 @@
     per, D = hidden.shape[1], hidden.shape[3]
     V = head_slices.shape[2]
     SEQ = seq_lengths.shape[0]
-    C, C2 = 4, 2
+    C, C2 = 1, 1
     TILE = min(512, D)
     R = PL * per
     Rp = -(-R // 128) * 128
@@ -408,9 +415,9 @@
     scores, adv, trunk = pl.pallas_call(
         functools.partial(kernel, (S, DP, MP, per, D, V, SEQ, C, C2, TILE)),
         out_shape=(
-            jax.ShapeDtypeStruct((1, per, 1), f32),
-            jax.ShapeDtypeStruct((per, 1), f32),
-            jax.ShapeDtypeStruct((per, D), bf16),
+            pltpu.VMEM((1, per), f32),
+            pltpu.VMEM((1, per), f32),
+            pltpu.VMEM((per, D), bf16),
         ),
         in_specs=[anym, vmem, pl.BlockSpec(memory_space=pltpu.SMEM), anym, vmem],
         out_specs=(vmem, vmem, vmem),
@@ -446,8 +453,8 @@
         compiler_params=pltpu.CompilerParams(
             collective_id=0, has_side_effects=True, vmem_limit_bytes=60 * 1024 * 1024
         ),
-    )(hidden.reshape(per, D), token_ids, seq_lengths, head_slices, value_head)
-    return scores, adv, trunk.reshape(1, per, 1, D)
+    )(hidden.reshape(per, D), token_ids.reshape(1, per), seq_lengths, head_slices, value_head)
+    return scores.reshape(1, per, 1), adv.reshape(per, 1), trunk.reshape(1, per, 1, D)
 
 
 def solution(mesh):

time: 35.2 us -> 28.4 us (0.81)
  local copies, waits for them, and re-layouts: 5.33 us -> 1.65 us
  Pallas kernels: 29 us -> 25.9 us
    unnamed x4 -> x3, local copies, waits for them, and re-layouts: 5.33 us -> 1.65 us
    pallas_call x1, Pallas kernels: 29 us -> 25.9 us  [local(): pl.pallas_call(functools.partial(kernel, (S, DP, MP, per, D, V, SEQ, C, C...]
where the time goes in v2:
time: 28.4 us; the launch traced here: 28.2 us
  Pallas kernels  25.9 us (91%)
  local copies, waits for them, and re-layouts  1.65 us (6%)
  between operations  0.64 us (2%)
    pallas_call x1, Pallas kernels, local(): pl.pallas_call(functools.partial(kernel, (S, DP, MP, per, D, V, SEQ, C, C...  25.9 us
    unnamed x3, local copies, waits for them, and re-layouts  1.65 us

profile of v2, /device:TPU:0, one launch (start us, length us, event | category | flops | bytes accessed | tf_op | source)
XLA Modules:
  0.0 28.2 jit_solution(9107000324055497345)
XLA Ops:
  0.6 25.9 %shard_map.76 = (f32[1,8]{1,0:T(1,128)S(1)}, f32[1,8]{1,0:T(1,128)S(1)}, bf16[8,4096]{1,0:T(8,128)(2,1)S(1)}) custom-call(bf16[8,4096]{1,0:T(8,128)(2,1)} %bitcast.8, s32[1,8]{1,0:T(1,128)} %bitcast.9, s32[4]{0:T(128)} %len_ref.1, bf16[1,4096,1024]{2,1,0:T(8,128)(2,1)} %head_ref.1, bf16[1,4096]{1,0:T(2,128)(2,1)} %vh_ref.1), custom_call_target="tpu_custom_call" | custom-call | tf_op jit(solution)/shard_map/pallas_call | solution.py:415
  26.6 0.5 %copy.11 = f32[1,8,1]{1,2,0:T(1,128)} copy(f32[1,8,1]{1,2,0:T(1,128)S(1)} %bitcast.7) | data formatting | bytes 64
  27.1 0.5 %copy.12 = f32[8,1]{0,1:T(1,128)} copy(f32[8,1]{0,1:T(1,128)S(1)} %bitcast.6) | data formatting | bytes 64
  27.6 0.6 %copy.13 = bf16[1,8,1,4096]{3,1,2,0:T(8,128)(2,1)} copy(bf16[1,8,1,4096]{3,1,2,0:T(8,128)(2,1)S(1)} %bitcast.5) | data formatting | bytes 131072

commit v3 on v2

--- a/solution.py
+++ b/solution.py
@@ -160,6 +160,9 @@
             for s in range(S - 1, 0, -1):
                 z_copy(c, s).start()
 
+        if c == 0:
+            each(PL, lambda o: tok_copy(o).start())
+
         @pl.when(sec != 0)
         def _():
             z_copy(c, 0).wait_recv()
@@ -187,8 +190,6 @@
     for step in range(C + 2):
         if step < C:
             spread(step)
-        if step == 0:
-            each(PL, lambda o: tok_copy(o).start())
         if 0 <= step - 1 < C:
             relay(step - 1)
         c = step - 2
@@ -394,6 +395,17 @@
     each(PL, lambda o: tok_copy(o).wait_send())
     each(PL, lambda o: stat_copy(o).wait_send())
     each(S, lambda o: zs_copy(o).wait_send())
+
+
+def hand_over(a_ref, b_ref, c_ref, a_out, b_out, c_out, sem):
+    moves = [
+        pltpu.make_async_copy(src, dst, sem.at[k])
+        for k, (src, dst) in enumerate(((a_ref, a_out), (b_ref, b_out), (c_ref, c_out)))
+    ]
+    for move in moves:
+        move.start()
+    for move in moves:
+        move.wait()
 
 
 def local(hidden, token_ids, seq_lengths, head_slices, value_head):
@@ -454,6 +466,17 @@
             collective_id=0, has_side_effects=True, vmem_limit_bytes=60 * 1024 * 1024
         ),
     )(hidden.reshape(per, D), token_ids.reshape(1, per), seq_lengths, head_slices, value_head)
+    scores, adv, trunk = pl.pallas_call(
+        hand_over,
+        out_shape=(
+            jax.ShapeDtypeStruct((1, per), f32),
+            jax.ShapeDtypeStruct((1, per), f32),
+            jax.ShapeDtypeStruct((per, D), bf16),
+        ),
+        in_specs=[vmem] * 3,
+        out_specs=[anym] * 3,
+        scratch_shapes=[dma((3,))],
+    )(*(pltpu.with_memory_space_constraint(v, pltpu.VMEM) for v in (scores, adv, trunk)))
     return scores.reshape(1, per, 1), adv.reshape(per, 1), trunk.reshape(1, per, 1, D)
 
 

time: 28.4 us -> 27.4 us (0.965)
  local copies, waits for them, and re-layouts: 1.65 us -> 0 us
  Pallas kernels: 25.9 us -> 26.6 us
    unnamed x3 -> x0, local copies, waits for them, and re-layouts: 1.65 us -> none
    pallas_call x0 -> x1, Pallas kernels: none -> 0.67 us  [local(): pl.pallas_call(hand_over, out_shape=(jax.ShapeDtypeStruct((1, per), f32),...]
where the time goes in v3:
time: 27.4 us; the launch traced here: 27.2 us
  Pallas kernels  26.6 us (97%)
  between operations  0.64 us (2%)
    pallas_call x1, Pallas kernels, local(): pl.pallas_call(functools.partial(kernel, (S, DP, MP, per, D, V, SEQ, C, C...  25.9 us
    pallas_call x1, Pallas kernels, local(): pl.pallas_call(hand_over, out_shape=(jax.ShapeDtypeStruct((1, per), f32),...  0.67 us

profile of v3, /device:TPU:0, one launch (start us, length us, event | category | flops | bytes accessed | tf_op | source)
XLA Modules:
  0.0 27.2 jit_solution(2733752024085387290)
XLA Ops:
  0.6 25.9 %shard_map.76 = (f32[1,8]{1,0:T(1,128)S(1)}, f32[1,8]{1,0:T(1,128)S(1)}, bf16[8,4096]{1,0:T(8,128)(2,1)S(1)}) custom-call(bf16[8,4096]{1,0:T(8,128)(2,1)} %bitcast.5, s32[1,8]{1,0:T(1,128)} %bitcast.6, s32[4]{0:T(128)} %len_ref.1, bf16[1,4096,1024]{2,1,0:T(8,128)(2,1)} %head_ref.1, bf16[1,4096]{1,0:T(2,128)(2,1)} %vh_ref.1), custom_call_target="tpu_custom_call" | custom-call | tf_op jit(solution)/shard_map/pallas_call | solution.py:427
  26.6 0.7 %shard_map.77 = (f32[1,8]{1,0:T(1,128)}, f32[1,8]{1,0:T(1,128)}, bf16[8,4096]{1,0:T(8,128)(2,1)}) custom-call(f32[1,8]{1,0:T(1,128)S(1)} %get-tuple-element.9.a_ref, f32[1,8]{1,0:T(1,128)S(1)} %get-tuple-element.10.b_ref, bf16[8,4096]{1,0:T(8,128)(2,1)S(1)} %get-tuple-element.11.c_ref), custom_call_target="tpu_custom_call" | custom-call | tf_op jit(solution)/shard_map/pallas_call | solution.py:469
